TPU v7x, 256 devices: a whole 4x4x8 slice. The times are simulated.
256 devices in a mesh: dp: 32 (over z_hi, x, core), seq: 8 (over y, z_lo).
Axes of the slice: x: 4, y: 4, z: 8 (z_hi: 4, z_lo: 2; z = z_hi * 2 + z_lo), core: 2. Of those that a mesh axis runs over, the one named last changes fastest.
Arguments:
- q_proj: bfloat16 [32, 1024, 4096], P('dp', 'seq'), may hold values from -200 to 200
- k_proj: bfloat16 [32, 1024, 512], P('dp', 'seq'), may hold values from -6 to 6
- v_proj: bfloat16 [32, 1024, 512], P('dp', 'seq'), may hold values from -6 to 6
- cache_k: bfloat16 [32, 1024, 512], P('dp', 'seq'), may hold values from -6 to 6
- cache_v: bfloat16 [32, 1024, 512], P('dp', 'seq'), may hold values from -6 to 6
- bias_q: bfloat16 [4096], replicated, may hold values from -3 to 3
- bias_k: bfloat16 [512], replicated, may hold values from -3 to 3
- bias_v: bfloat16 [512], replicated, may hold values from -3 to 3
- start: int32 [32], P('dp'), may hold values from 256 to 1024, as said below
- dout: bfloat16 [32, 1024, 4096], P('dp', 'seq'), may hold values from -6 to 6
Outputs:
- attn_out: bfloat16 [32, 1024, 4096], P('dp', 'seq')
- grad_q: bfloat16 [32, 1024, 4096], P('dp', 'seq')
- grad_k: bfloat16 [32, 1024, 512], P('dp', 'seq')
- grad_v: bfloat16 [32, 1024, 512], P('dp', 'seq')
- grad_bias_q: float32 [4096], replicated
- grad_bias_k: float32 [512], replicated
- grad_bias_v: float32 [512], replicated
Inputs may be any that keep to these rules, and one draw needn't show every extreme that they name: Cache slots at and beyond start hold no prefix; some sequence has a full prefix of 1024 slots.
All inputs are finite; a program needn't handle non-finite values.
Results may differ from a plain program's by a relative error of at most 0.04.
The roundings to bfloat16 on the way count: a program that leaves them out, or rounds other values in their place, can miss the bound.
Values may be sent and summed in bfloat16 or wider, within the bound.
A program may use at most 128 MiB of HBM per device.

v0:
```python
import jax
import jax.numpy as jnp
from jax import lax
from jax.sharding import PartitionSpec as P

HQ = 32
KV = 4
HD = 128
GROUP = 8


def rotary_tables(positions, width):
    half = width // 2
    freqs = jnp.exp(
        -(2.0 * jnp.arange(half, dtype=jnp.float32) / width) * jnp.log(jnp.float32(1000000.0))
    )
    angles = positions.astype(jnp.float32)[:, None] * freqs[None, :]
    cosine = jnp.concatenate([jnp.cos(angles), jnp.cos(angles)], axis=1)
    sine = jnp.concatenate([jnp.sin(angles), jnp.sin(angles)], axis=1)
    return (cosine[:, None, :], sine[:, None, :])


def rotary(values, positions):
    cosine, sine = rotary_tables(positions, values.shape[2])
    half = values.shape[2] // 2
    turned = jnp.concatenate([-values[:, :, half:], values[:, :, :half]], axis=2)
    return values * cosine + turned * sine


def rotary_back(grads, positions):
    cosine, sine = rotary_tables(positions, grads.shape[2])
    half = grads.shape[2] // 2
    scaled = grads * sine
    turned = jnp.concatenate([scaled[:, :, half:], -scaled[:, :, :half]], axis=2)
    return grads * cosine + turned


def attend(queries, cotangent, keys, values, first, row_zero, prefix):
    rows, heads, width = queries.shape
    key_count = keys.shape[0]
    slab = key_count - prefix
    head_block = max(1, min(512 // rows, GROUP, heads))
    row_block = min(rows, 512)
    scale = width ** (-0.5)
    key_index = jnp.arange(key_count, dtype=jnp.int32)

    def head_step(carry, head_slot):
        key_acc, value_acc = carry
        head_zero = head_slot * head_block
        owner = head_zero // GROUP
        key_one = lax.dynamic_index_in_dim(keys, owner, 1, keepdims=False)
        value_one = lax.dynamic_index_in_dim(values, owner, 1, keepdims=False)
        query_part = lax.dynamic_slice_in_dim(queries, head_zero, head_block, 1)
        cot_part = lax.dynamic_slice_in_dim(cotangent, head_zero, head_block, 1)

        def row_step(inner, row_slot):
            grad_key, grad_value = inner
            offset = row_slot * row_block
            query_rows = lax.dynamic_slice_in_dim(query_part, offset, row_block, 0)
            cot_rows = lax.dynamic_slice_in_dim(cot_part, offset, row_block, 0)
            query_index = row_zero + offset + jnp.arange(row_block, dtype=jnp.int32)
            allowed = jnp.where(
                key_index[None, :] < prefix,
                key_index[None, :] < first,
                key_index[None, :] - prefix <= query_index[:, None],
            )
            scores = (
                jnp.einsum("rhd,kd->hrk", query_rows, key_one, preferred_element_type=jnp.float32)
                * scale
            )
            scores = jnp.where(allowed[None], scores, -1e30)
            highest = jnp.max(scores, axis=-1, keepdims=True)
            expo = jnp.exp(scores - highest)
            probs = expo / jnp.sum(expo, axis=-1, keepdims=True)
            probs_b = probs.astype(jnp.bfloat16)
            output = jnp.einsum(
                "hrk,kd->rhd", probs_b, value_one, preferred_element_type=jnp.float32
            ).astype(jnp.bfloat16)
            delta = jnp.sum(cot_rows.astype(jnp.float32) * output.astype(jnp.float32), axis=-1).T
            dprobs = jnp.einsum(
                "rhd,kd->hrk", cot_rows, value_one, preferred_element_type=jnp.float32
            )
            dscore = (probs * (dprobs - delta[:, :, None])).astype(jnp.bfloat16)
            grad_query = (
                jnp.einsum("hrk,kd->rhd", dscore, key_one, preferred_element_type=jnp.float32)
                * scale
            ).astype(jnp.bfloat16)
            grad_key = (
                grad_key
                + jnp.einsum(
                    "hrk,rhd->kd",
                    dscore[:, :, prefix:],
                    query_rows,
                    preferred_element_type=jnp.float32,
                )
                * scale
            )
            grad_value = grad_value + jnp.einsum(
                "hrk,rhd->kd", probs_b[:, :, prefix:], cot_rows, preferred_element_type=jnp.float32
            )
            return ((grad_key, grad_value), (output, grad_query))

        empty = jnp.zeros((slab, width), jnp.float32)
        (grad_key, grad_value), (outputs, grads) = lax.scan(
            row_step, (empty, empty), jnp.arange(rows // row_block, dtype=jnp.int32)
        )
        outputs = outputs.reshape(rows, head_block, width)
        grads = grads.reshape(rows, head_block, width)
        old_key = lax.dynamic_index_in_dim(key_acc, owner, 1, keepdims=False)
        old_value = lax.dynamic_index_in_dim(value_acc, owner, 1, keepdims=False)
        key_acc = lax.dynamic_update_index_in_dim(key_acc, old_key + grad_key, owner, 1)
        value_acc = lax.dynamic_update_index_in_dim(value_acc, old_value + grad_value, owner, 1)
        return ((key_acc, value_acc), (outputs, grads))

    zeros_kv = jnp.zeros((slab, keys.shape[1], width), jnp.float32)
    (key_acc, value_acc), (outputs, grads) = lax.scan(
        head_step, (zeros_kv, zeros_kv), jnp.arange(heads // head_block, dtype=jnp.int32)
    )
    outputs = jnp.transpose(outputs, (1, 0, 2, 3)).reshape(rows, heads, width)
    grads = jnp.transpose(grads, (1, 0, 2, 3)).reshape(rows, heads, width)
    return (outputs, grads, key_acc, value_acc)


def body(q_proj, k_proj, v_proj, cache_k, cache_v, bias_q, bias_k, bias_v, start, dout):
    devices = lax.axis_size("seq")
    rank = lax.axis_index("seq")
    tokens = q_proj.shape[1]
    first = start[0]
    positions = first + rank * tokens + jnp.arange(tokens, dtype=jnp.int32)
    queries = rotary(
        (q_proj[0].astype(jnp.float32) + bias_q.astype(jnp.float32)).reshape(tokens, HQ, HD),
        positions,
    ).astype(jnp.bfloat16)
    keys = rotary(
        (k_proj[0].astype(jnp.float32) + bias_k.astype(jnp.float32)).reshape(tokens, KV, HD),
        positions,
    ).astype(jnp.bfloat16)
    values = (
        (v_proj[0].astype(jnp.float32) + bias_v.astype(jnp.float32))
        .astype(jnp.bfloat16)
        .reshape(tokens, KV, HD)
    )
    cotangent = dout[0].reshape(tokens, HQ, HD)
    cached_keys = cache_k[0].reshape(cache_k.shape[1], KV, HD)
    cached_values = cache_v[0].reshape(cache_v.shape[1], KV, HD)
    copies = max(devices // KV, 1)
    keys_wide = jnp.repeat(keys, copies, axis=1)
    values_wide = jnp.repeat(values, copies, axis=1)
    cache_keys_wide = jnp.repeat(cached_keys, copies, axis=1)
    cache_values_wide = jnp.repeat(cached_values, copies, axis=1)
    head_queries, head_keys, head_values, head_cot = (
        lax.all_to_all(queries, "seq", split_axis=1, concat_axis=0, tiled=True),
        lax.all_to_all(keys_wide, "seq", split_axis=1, concat_axis=0, tiled=True),
        lax.all_to_all(values_wide, "seq", split_axis=1, concat_axis=0, tiled=True),
        lax.all_to_all(cotangent, "seq", split_axis=1, concat_axis=0, tiled=True),
    )
    head_cache_keys, head_cache_values = (
        lax.all_to_all(cache_keys_wide, "seq", split_axis=1, concat_axis=0, tiled=True),
        lax.all_to_all(cache_values_wide, "seq", split_axis=1, concat_axis=0, tiled=True),
    )
    prefix = head_cache_keys.shape[0]
    all_keys = jnp.concatenate([head_cache_keys, head_keys], axis=0)
    all_values = jnp.concatenate([head_cache_values, head_values], axis=0)
    outputs, dq_rot, dk_rot, dv_all = attend(
        head_queries, head_cot, all_keys, all_values, first, 0, prefix
    )
    out_tokens, dq_tokens = (
        lax.all_to_all(outputs, "seq", split_axis=0, concat_axis=1, tiled=True),
        lax.all_to_all(dq_rot, "seq", split_axis=0, concat_axis=1, tiled=True),
    )
    dk_copies, dv_copies = (
        lax.all_to_all(
            dk_rot.astype(jnp.bfloat16), "seq", split_axis=0, concat_axis=1, tiled=True
        ).astype(dk_rot.dtype),
        lax.all_to_all(
            dv_all.astype(jnp.bfloat16), "seq", split_axis=0, concat_axis=1, tiled=True
        ).astype(dv_all.dtype),
    )
    dk_tokens = jnp.sum(dk_copies.reshape(tokens, KV, copies, HD), axis=2)
    dv_tokens = jnp.sum(dv_copies.reshape(tokens, KV, copies, HD), axis=2)
    grad_query = rotary_back(dq_tokens.astype(jnp.float32), positions)
    grad_key = rotary_back(dk_tokens, positions)
    sums_query, sums_key, sums_value = lax.psum(
        (
            jnp.sum(grad_query, axis=0).reshape(HQ * HD),
            jnp.sum(grad_key, axis=0).reshape(KV * HD),
            jnp.sum(dv_tokens, axis=0).reshape(KV * HD),
        ),
        ("dp", "seq"),
    )
    return (
        out_tokens.reshape(1, tokens, HQ * HD),
        grad_query.astype(jnp.bfloat16).reshape(1, tokens, HQ * HD),
        grad_key.astype(jnp.bfloat16).reshape(1, tokens, KV * HD),
        dv_tokens.astype(jnp.bfloat16).reshape(1, tokens, KV * HD),
        sums_query,
        sums_key,
        sums_value,
    )


def solution(mesh):
    placed = (
        P("dp", "seq", None),
        P("dp", "seq", None),
        P("dp", "seq", None),
        P("dp", "seq", None),
        P("dp", "seq", None),
        P(),
        P(),
        P(),
        P("dp"),
        P("dp", "seq", None),
    )
    return jax.shard_map(
        body,
        mesh=mesh,
        in_specs=placed,
        out_specs=(
            P("dp", "seq", None),
            P("dp", "seq", None),
            P("dp", "seq", None),
            P("dp", "seq", None),
            P(),
            P(),
            P(),
        ),
        check_vma=False,
    )
```

profile of v0, /device:TPU:1, one launch (start us, length us, event | category | flops | bytes accessed | tf_op | source)
XLA Modules:
  0.0 376.5 jit_solution(17324488417311112449)
XLA Ops:
  2.4 6.5 %all-to-all-start.2 = ((bf16[128,8,128]{2,0,1:T(8,128)(2,1)}), bf16[128,8,128]{2,0,1:T(8,128)(2,1)S(1)}, u32[]{:S(2)}, u32[]{:S(2)}) async-start(bf16[128,8,128]{2,0,1:T(8,128)(2,1)} %bitcast.11), calls=%async_computation.2 | async-start | bytes 524288 | tf_op jit(solution)/shard_map/all_to_all | solution.py:158
  15.8 3.4 all-to-all-start.4
  19.3 6.0 %all-to-all-done.4 = bf16[128,8,128]{2,0,1:T(8,128)(2,1)S(1)} async-done(((bf16[128,8,128]{2,0,1:T(8,128)(2,1)}), bf16[128,8,128]{2,0,1:T(8,128)(2,1)S(1)}, u32[]{:S(2)}, u32[]{:S(2)}) %all-to-all-start.4) | async-done | bytes 262176 | tf_op jit(solution)/shard_map/all_to_all | solution.py:159
  26.1 3.4 all-to-all-start.5
  29.8 5.8 %all-to-all-done.5 = bf16[128,8,128]{2,0,1:T(8,128)(2,1)S(1)} async-done(((bf16[128,8,128]{2,0,1:T(8,128)(2,1)}), bf16[128,8,128]{2,0,1:T(8,128)(2,1)S(1)}, u32[]{:S(2)}, u32[]{:S(2)}) %all-to-all-start.5) | async-done | bytes 262176 | tf_op jit(solution)/shard_map/all_to_all | solution.py:154
  36.4 3.4 all-to-all-start.3
  41.2 4.7 %all-to-all-done.3 = bf16[128,8,128]{2,0,1:T(8,128)(2,1)S(1)} async-done(((bf16[128,8,128]{2,0,1:T(8,128)(2,1)}), bf16[128,8,128]{2,0,1:T(8,128)(2,1)S(1)}, u32[]{:S(2)}, u32[]{:S(2)}) %all-to-all-start.3) | async-done | bytes 262176 | tf_op jit(solution)/shard_map/all_to_all | solution.py:153
  45.9 3.7 all-to-all-start.1
  53.5 6.5 %all-to-all-done.1 = bf16[128,32,128]{0,2,1:T(8,128)(2,1)S(1)} async-done(((bf16[128,32,128]{0,2,1:T(8,128)(2,1)}), bf16[128,32,128]{0,2,1:T(8,128)(2,1)S(1)}, u32[]{:S(2)}, u32[]{:S(2)}) %all-to-all-start.1) | async-done | bytes 1048608 | tf_op jit(solution)/shard_map/all_to_all | solution.py:155
  60.0 3.6 all-to-all-start
  66.7 7.2 %all-to-all-done = bf16[128,32,128]{2,0,1:T(8,128)(2,1)S(1)} async-done(((bf16[128,32,128]{2,0,1:T(8,128)(2,1)}), bf16[128,32,128]{2,0,1:T(8,128)(2,1)S(1)}, u32[]{:S(2)}, u32[]{:S(2)}) %all-to-all-start) | async-done | bytes 1048608 | tf_op jit(solution)/shard_map/all_to_all | solution.py:152
  75.0 139.6 %while.59 = (s32[]{:T(128)}, f32[1024,1,128]{2,0,1:T(8,128)S(1)}, f32[1024,1,128]{2,0,1:T(8,128)S(1)}, bf16[4,1024,1,128]{3,1,2,0:T(8,128)(2,1)}, bf16[4,1024,1,...) while((s32[]{:T(128)}, f32[1024,1,128]{2,0,1:T(8,128)S(1)}, ...), condition=%wide.region_6.7_spmd.clone.clone, body=%wide.region_0.6_spmd.clone.clone.sunk | while | flops 1359287296 | bytes 49224388 | solution.py:116
  79.6 28.5 %while.60 = (s32[]{:T(128)}, f32[1024,128]{1,0:T(8,128)S(1)}, f32[1024,128]{1,0:T(8,128)S(1)}, bf16[2,512,1,128]{3,1,0,2:T(8,128)(2,1)}, bf16[2,512,1,128]{3,1,2...) while((s32[]{:T(128)}, f32[1024,128]{1,0:T(8,128)S(1)}, ...), condition=%wide.region_5.5_spmd.clone.clone, body=%wide.region_1.4_spmd.clone.clone.sunk | while | flops 1359025152 | bytes 41875732 | solution.py:104
  90.1 3.1 fusion.81
  104.4 3.1 fusion.81
  114.5 28.5 %while.60 = (s32[]{:T(128)}, f32[1024,128]{1,0:T(8,128)S(1)}, f32[1024,128]{1,0:T(8,128)S(1)}, bf16[2,512,1,128]{3,1,0,2:T(8,128)(2,1)}, bf16[2,512,1,128]{3,1,2...) while((s32[]{:T(128)}, f32[1024,128]{1,0:T(8,128)S(1)}, ...), condition=%wide.region_5.5_spmd.clone.clone, body=%wide.region_1.4_spmd.clone.clone.sunk | while | flops 1359025152 | bytes 41875732 | solution.py:104
  125.0 3.1 fusion.81
  139.3 3.1 fusion.81
  149.4 28.5 %while.60 = (s32[]{:T(128)}, f32[1024,128]{1,0:T(8,128)S(1)}, f32[1024,128]{1,0:T(8,128)S(1)}, bf16[2,512,1,128]{3,1,0,2:T(8,128)(2,1)}, bf16[2,512,1,128]{3,1,2...) while((s32[]{:T(128)}, f32[1024,128]{1,0:T(8,128)S(1)}, ...), condition=%wide.region_5.5_spmd.clone.clone, body=%wide.region_1.4_spmd.clone.clone.sunk | while | flops 1359025152 | bytes 41875732 | solution.py:104
  174.2 3.1 fusion.81
  184.3 28.5 %while.60 = (s32[]{:T(128)}, f32[1024,128]{1,0:T(8,128)S(1)}, f32[1024,128]{1,0:T(8,128)S(1)}, bf16[2,512,1,128]{3,1,0,2:T(8,128)(2,1)}, bf16[2,512,1,128]{3,1,2...) while((s32[]{:T(128)}, f32[1024,128]{1,0:T(8,128)S(1)}, ...), condition=%wide.region_5.5_spmd.clone.clone, body=%wide.region_1.4_spmd.clone.clone.sunk | while | flops 1359025152 | bytes 41875732 | solution.py:104
  209.1 3.1 fusion.81
  216.8 3.4 all-to-all-start.8
  221.8 4.5 %all-to-all-done.8 = bf16[8,2,8192]{2,1,0:T(2,128)(2,1)S(1)} async-done(((bf16[8,2,8192]{2,1,0:T(2,128)(2,1)}), bf16[8,2,8192]{2,1,0:T(2,128)(2,1)S(1)}, u32[]{:S(2)}, u32[]{:S(2)}) %all-to-all-start.8) | async-done | bytes 262176 | tf_op jit(solution)/shard_map/all_to_all | solution.py:172
  226.3 3.6 all-to-all-start.9
  229.9 3.1 copy.153
  233.0 3.2 all-to-all-done.9
  236.2 3.6 all-to-all-start.6
  241.6 9.9 %all-to-all-done.6 = bf16[1024,4,128]{2,1,0:T(4,128)(2,1)S(1)} async-done(((bf16[1024,4,128]{2,1,0:T(4,128)(2,1)}), bf16[1024,4,128]{2,1,0:T(4,128)(2,1)S(1)}, u32[]{:S(2)}, u32[]{:S(2)}) %all-to-all-start.6) | async-done | bytes 1048608 | tf_op jit(solution)/shard_map/all_to_all | solution.py:168
  251.5 3.6 all-to-all-start.7
  273.0 3.2 copy.163
  286.0 90.5 %all-reduce = (f32[4096]{0:T(1024)}, f32[512]{0:T(512)}, f32[512]{0:T(512)}) all-reduce(f32[4096]{0:T(1024)S(1)} %bitcast.274, f32[512]{0:T(512)S(1)} %bitcast.276, f32[512]{0:T(512)S(1)} %bitcast.277), channel_id=1, replica_groups=mesh['dp'=32,'seq'=8] {'dp','seq'}, use_global_device_ids=true, to_apply=%region_10.11 | all-reduce | flops 5120 | bytes 40960 | tf_op jit(solution)/shard_map/psum | solution.py:183
  (322 shorter events, 159.2 us)
Async XLA Ops:
  0.6 10.7 %copy-start.22 = (bf16[1,128,512]{2,1,0:T(8,128)(2,1)S(1)}, bf16[1,128,512]{2,1,0:T(8,128)(2,1)}, u32[]{:S(2)}) copy-start(bf16[1,128,512]{2,1,0:T(8,128)(2,1)} %param.15) | copy-start | bytes 393220
  0.6 10.9 %copy-start.23 = (bf16[1,128,512]{2,1,0:T(8,128)(2,1)S(1)}, bf16[1,128,512]{2,1,0:T(8,128)(2,1)}, u32[]{:S(2)}) copy-start(bf16[1,128,512]{2,1,0:T(8,128)(2,1)} %param.18) | copy-start | bytes 393220
  2.4 16.9 %copy-start.25 = (bf16[512]{0:T(512)(128)(2,1)S(1)}, bf16[512]{0:T(512)(128)(2,1)}, u32[]{:S(2)}) copy-start(bf16[512]{0:T(512)(128)(2,1)} %param.20) | copy-start | bytes 3076
  2.4 12.7 %all-to-all-start.2 = ((bf16[128,8,128]{2,0,1:T(8,128)(2,1)}), bf16[128,8,128]{2,0,1:T(8,128)(2,1)S(1)}, u32[]{:S(2)}, u32[]{:S(2)}) async-start(bf16[128,8,128]{2,0,1:T(8,128)(2,1)} %bitcast.11), calls=%async_computation.2 | async-start | bytes 524288 | tf_op jit(solution)/shard_map/all_to_all | solution.py:158
  12.1 37.5 %copy-start.8 = (f32[128,128]{1,0:T(8,128)}, f32[128,128]{1,0:T(8,128)S(1)}, u32[]{:S(2)}) copy-start(f32[128,128]{1,0:T(8,128)S(1)} %get-tuple-element.735) | copy-start | bytes 196612
  12.1 37.6 %copy-start.6 = (f32[128,128]{1,0:T(8,128)}, f32[128,128]{1,0:T(8,128)S(1)}, u32[]{:S(2)}) copy-start(f32[128,128]{1,0:T(8,128)S(1)} %get-tuple-element.734) | copy-start | bytes 196612
  15.8 9.5 %all-to-all-start.4 = ((bf16[128,8,128]{2,0,1:T(8,128)(2,1)}), bf16[128,8,128]{2,0,1:T(8,128)(2,1)S(1)}, u32[]{:S(2)}, u32[]{:S(2)}) async-start(bf16[128,8,128]{2,0,1:T(8,128)(2,1)} %bitcast.21), calls=%async_computation.4 | async-start | bytes 524288 | tf_op jit(solution)/shard_map/all_to_all | solution.py:159
  19.3 20.5 %copy-start.10 = (bf16[1,128,4096]{2,1,0:T(8,128)(2,1)S(1)}, bf16[1,128,4096]{2,1,0:T(8,128)(2,1)}, u32[]{:S(2)}) copy-start(bf16[1,128,4096]{2,1,0:T(8,128)(2,1)} %param.23) | copy-start | bytes 3145732
  25.3 15.8 %copy-start.13 = (bf16[128,8,128]{2,0,1:T(8,128)(2,1)}, bf16[128,8,128]{2,0,1:T(8,128)(2,1)S(1)}, u32[]{:S(2)}) copy-start(bf16[128,8,128]{2,0,1:T(8,128)(2,1)S(1)} %all-to-all-done.4) | copy-start | bytes 786436
  26.1 9.5 %all-to-all-start.5 = ((bf16[128,8,128]{2,0,1:T(8,128)(2,1)}), bf16[128,8,128]{2,0,1:T(8,128)(2,1)S(1)}, u32[]{:S(2)}, u32[]{:S(2)}) async-start(bf16[128,8,128]{2,0,1:T(8,128)(2,1)} %bitcast.26), calls=%async_computation.5 | async-start | bytes 524288 | tf_op jit(solution)/shard_map/all_to_all | solution.py:154
  36.4 9.5 %all-to-all-start.3 = ((bf16[128,8,128]{2,0,1:T(8,128)(2,1)}), bf16[128,8,128]{2,0,1:T(8,128)(2,1)S(1)}, u32[]{:S(2)}, u32[]{:S(2)}) async-start(bf16[128,8,128]{2,0,1:T(8,128)(2,1)} %bitcast.17), calls=%async_computation.3 | async-start | bytes 524288 | tf_op jit(solution)/shard_map/all_to_all | solution.py:153
  39.8 10.0 %copy-start.11 = (bf16[1,128,4096]{2,1,0:T(8,128)(2,1)S(1)}, bf16[1,128,4096]{2,1,0:T(8,128)(2,1)}, u32[]{:S(2)}) copy-start(bf16[1,128,4096]{2,1,0:T(8,128)(2,1)} %param.14) | copy-start | bytes 3145732
  45.9 3.8 %copy-start.17 = (bf16[128,8,128]{2,0,1:T(8,128)(2,1)}, bf16[128,8,128]{2,0,1:T(8,128)(2,1)S(1)}, u32[]{:S(2)}) copy-start(bf16[128,8,128]{2,0,1:T(8,128)(2,1)S(1)} %all-to-all-done.3) | copy-start | bytes 786436
  45.9 4.6 %copy-start.24 = (bf16[4096]{0:T(1024)(128)(2,1)S(1)}, bf16[4096]{0:T(1024)(128)(2,1)}, u32[]{:S(2)}) copy-start(bf16[4096]{0:T(1024)(128)(2,1)} %param.19) | copy-start | bytes 24580
  45.9 14.1 %all-to-all-start.1 = ((bf16[128,32,128]{0,2,1:T(8,128)(2,1)}), bf16[128,32,128]{0,2,1:T(8,128)(2,1)S(1)}, u32[]{:S(2)}, u32[]{:S(2)}) async-start(bf16[128,32,128]{0,2,1:T(8,128)(2,1)} %bitcast.6), calls=%async_computation.1 | async-start | bytes 2097152 | tf_op jit(solution)/shard_map/all_to_all | solution.py:155
  52.2 11.4 %copy-start.14 = (bf16[128,8,128]{2,0,1:T(8,128)(2,1)S(1)}, bf16[128,8,128]{2,0,1:T(8,128)(2,1)}, u32[]{:S(2)}) copy-start(bf16[128,8,128]{2,0,1:T(8,128)(2,1)} %copy-done.13) | copy-start | bytes 786436
  52.2 11.4 %copy-start.16 = (bf16[128,8,128]{2,0,1:T(8,128)(2,1)S(1)}, bf16[128,8,128]{2,0,1:T(8,128)(2,1)}, u32[]{:S(2)}) copy-start(bf16[128,8,128]{2,0,1:T(8,128)(2,1)} %copy-done.15) | copy-start | bytes 786436
  60.0 13.9 %all-to-all-start = ((bf16[128,32,128]{2,0,1:T(8,128)(2,1)}), bf16[128,32,128]{2,0,1:T(8,128)(2,1)S(1)}, u32[]{:S(2)}, u32[]{:S(2)}) async-start(bf16[128,32,128]{2,0,1:T(8,128)(2,1)} %copy.142), calls=%async_computation | async-start | bytes 2097152 | tf_op jit(solution)/shard_map/all_to_all | solution.py:152
  89.4 3.7 copy-start
  103.7 3.8 copy-start
  124.3 3.7 copy-start
  138.6 3.8 copy-start
  159.3 3.7 copy-start
  173.5 3.8 copy-start
  194.2 3.7 copy-start
  208.4 3.8 copy-start
  216.8 9.5 %all-to-all-start.8 = ((bf16[8,2,8192]{2,1,0:T(2,128)(2,1)}), bf16[8,2,8192]{2,1,0:T(2,128)(2,1)S(1)}, u32[]{:S(2)}, u32[]{:S(2)}) async-start(bf16[8,2,8192]{2,1,0:T(2,128)(2,1)} %reshape.436), calls=%async_computation.8 | async-start | bytes 524288 | tf_op jit(solution)/shard_map/all_to_all | solution.py:172
  226.3 10.0 %all-to-all-start.9 = ((bf16[8,2,8192]{2,1,0:T(2,128)(2,1)}), bf16[8,2,8192]{2,1,0:T(2,128)(2,1)S(1)}, u32[]{:S(2)}, u32[]{:S(2)}) async-start(bf16[8,2,8192]{2,1,0:T(2,128)(2,1)} %reshape.438), calls=%async_computation.9 | async-start | bytes 524288 | tf_op jit(solution)/shard_map/all_to_all | solution.py:175
  229.9 9.9 %copy-start.12 = (bf16[4,1024,1,128]{3,1,2,0:T(8,128)(2,1)S(1)}, bf16[4,1024,1,128]{3,1,2,0:T(8,128)(2,1)}, u32[]{:S(2)}) copy-start(bf16[4,1024,1,128]{3,1,2,0:T(8,128)(2,1)} %get-tuple-element.348) | copy-start | bytes 3145732
  236.2 15.3 %all-to-all-start.6 = ((bf16[1024,4,128]{2,1,0:T(4,128)(2,1)}), bf16[1024,4,128]{2,1,0:T(4,128)(2,1)S(1)}, u32[]{:S(2)}, u32[]{:S(2)}) async-start(bf16[1024,4,128]{2,1,0:T(4,128)(2,1)} %copy.153), calls=%async_computation.6 | async-start | bytes 2097152 | tf_op jit(solution)/shard_map/all_to_all | solution.py:168
  251.5 16.6 %all-to-all-start.7 = ((bf16[1024,4,128]{2,1,0:T(4,128)(2,1)}), bf16[1024,4,128]{2,1,0:T(4,128)(2,1)S(1)}, u32[]{:S(2)}, u32[]{:S(2)}) async-start(bf16[1024,4,128]{2,1,0:T(4,128)(2,1)} %bitcast.260), calls=%async_computation.7 | async-start | bytes 2097152 | tf_op jit(solution)/shard_map/all_to_all | solution.py:169
  255.4 5.0 %copy-start.9 = (f32[128,128]{1,0:T(8,128)S(1)}, f32[128,128]{1,0:T(8,128)}, u32[]{:S(2)}) copy-start(f32[128,128]{1,0:T(8,128)} %copy-done.8) | copy-start | bytes 196612
  (17 other events, 30.5 us)
where the time goes:
time: 379 us; the launch traced here: 376 us
  blocking collectives  90.5 us (24%)
  matrix products  79 us (21%)
  local copies, waits for them, and re-layouts  62 us (16%)
  waiting for transfers between devices  53.1 us (14%)
  starting transfers between devices  38.1 us (10%)
  other arithmetic  37.6 us (10%)
  loops' own time  14.1 us (4%)
    psum x1, blocking collectives, body(): lax.psum((jnp.sum(grad_query, axis=0).reshape(HQ * HD), jnp.sum(grad_key,...  90.5 us
    dot_general x8, matrix products, row_step(): jnp.einsum('hrk,kd->rhd', dscore, key_one, preferred_element_type=jnp.flo...  24.6 us
    dot_general x8, matrix products, row_step(): jnp.einsum('rhd,kd->hrk', cot_rows, value_one, preferred_element_type=jnp...  19.4 us
    dot_general x8, matrix products, row_step(): jnp.einsum('rhd,kd->hrk', query_rows, key_one, preferred_element_type=jnp...  18.6 us
    all_to_all x1, waiting for transfers between devices, body(): lax.all_to_all(outputs, 'seq', split_axis=0, concat_axis=1, tiled=True)  9.94 us
    another operation x1, loops' own time, attend(): lax.scan(head_step, (zeros_kv, zeros_kv), jnp.arange(heads // head_block,...  8.13 us
    unnamed x57, local copies, waits for them, and re-layouts  7.6 us
  transfers between devices with their start and end apart: 10, of which 10 were waited for; matrix products, arithmetic and copies ran while one was open for 7% of the time, Pallas kernels for 0%

commit v1 on v0

--- a/solution.py
+++ b/solution.py
@@ -181,12 +181,15 @@
     grad_query = rotary_back(dq_tokens.astype(jnp.float32), positions)
     grad_key = rotary_back(dk_tokens, positions)
     sums_query, sums_key, sums_value = lax.psum(
-        (
-            jnp.sum(grad_query, axis=0).reshape(HQ * HD),
-            jnp.sum(grad_key, axis=0).reshape(KV * HD),
-            jnp.sum(dv_tokens, axis=0).reshape(KV * HD),
+        lax.psum(
+            (
+                jnp.sum(grad_query, axis=0).reshape(HQ * HD),
+                jnp.sum(grad_key, axis=0).reshape(KV * HD),
+                jnp.sum(dv_tokens, axis=0).reshape(KV * HD),
+            ),
+            "dp",
         ),
-        ("dp", "seq"),
+        "seq",
     )
     return (
         out_tokens.reshape(1, tokens, HQ * HD),

time: 379 us -> 473 us (1.25)
  the two profiles are of different devices: /device:TPU:1 before, /device:TPU:0 now
where the time goes in v1:
time: 473 us; the launch traced here: 471 us
  blocking collectives  174 us (37%)
  matrix products  78.9 us (17%)
  waiting for transfers between devices  65.3 us (14%)
  local copies, waits for them, and re-layouts  62 us (13%)
  other arithmetic  37.6 us (8%)
  starting transfers between devices  36.2 us (8%)
  loops' own time  14.1 us (3%)
    psum x1, blocking collectives, body(): lax.psum((jnp.sum(grad_query, axis=0).reshape(HQ * HD), jnp.sum(grad_key,...  140 us
    psum x1, blocking collectives, body(): lax.psum(lax.psum((jnp.sum(grad_query, axis=0).reshape(HQ * HD), jnp.sum(...  34.5 us
    dot_general x8, matrix products, row_step(): jnp.einsum('hrk,kd->rhd', dscore, key_one, preferred_element_type=jnp.flo...  24.6 us
    dot_general x8, matrix products, row_step(): jnp.einsum('rhd,kd->hrk', cot_rows, value_one, preferred_element_type=jnp...  19.3 us
    dot_general x8, matrix products, row_step(): jnp.einsum('rhd,kd->hrk', query_rows, key_one, preferred_element_type=jnp...  18.5 us
    all_to_all x1, waiting for transfers between devices, body(): lax.all_to_all(outputs, 'seq', split_axis=0, concat_axis=1, tiled=True)  12.6 us
  transfers between devices with their start and end apart: 10, of which 10 were waited for; matrix products, arithmetic and copies ran while one was open for 6% of the time, Pallas kernels for 0%

profile of v1, /device:TPU:0, one launch (start us, length us, event | category | flops | bytes accessed | tf_op | source)
XLA Modules:
  0.0 470.5 jit_solution(18312971573839053873)
XLA Ops:
  2.4 4.2 all-to-all-start.2
  9.8 4.1 all-to-all-done.2
  14.6 3.4 all-to-all-start.4
  18.1 7.2 %all-to-all-done.4 = bf16[128,8,128]{2,0,1:T(8,128)(2,1)S(1)} async-done(((bf16[128,8,128]{2,0,1:T(8,128)(2,1)}), bf16[128,8,128]{2,0,1:T(8,128)(2,1)S(1)}, u32[]{:S(2)}, u32[]{:S(2)}) %all-to-all-start.4) | async-done | bytes 262176 | tf_op jit(solution)/shard_map/all_to_all | solution.py:159
  26.1 3.4 all-to-all-start.5
  29.8 6.9 %all-to-all-done.5 = bf16[128,8,128]{2,0,1:T(8,128)(2,1)S(1)} async-done(((bf16[128,8,128]{2,0,1:T(8,128)(2,1)}), bf16[128,8,128]{2,0,1:T(8,128)(2,1)S(1)}, u32[]{:S(2)}, u32[]{:S(2)}) %all-to-all-start.5) | async-done | bytes 262176 | tf_op jit(solution)/shard_map/all_to_all | solution.py:154
  37.5 3.4 all-to-all-start.3
  42.3 5.9 %all-to-all-done.3 = bf16[128,8,128]{2,0,1:T(8,128)(2,1)S(1)} async-done(((bf16[128,8,128]{2,0,1:T(8,128)(2,1)}), bf16[128,8,128]{2,0,1:T(8,128)(2,1)S(1)}, u32[]{:S(2)}, u32[]{:S(2)}) %all-to-all-start.3) | async-done | bytes 262176 | tf_op jit(solution)/shard_map/all_to_all | solution.py:153
  48.2 3.7 all-to-all-start.1
  55.8 7.9 %all-to-all-done.1 = bf16[128,32,128]{0,2,1:T(8,128)(2,1)S(1)} async-done(((bf16[128,32,128]{0,2,1:T(8,128)(2,1)}), bf16[128,32,128]{0,2,1:T(8,128)(2,1)S(1)}, u32[]{:S(2)}, u32[]{:S(2)}) %all-to-all-start.1) | async-done | bytes 1048608 | tf_op jit(solution)/shard_map/all_to_all | solution.py:155
  63.7 3.6 all-to-all-start
  70.4 8.3 %all-to-all-done = bf16[128,32,128]{2,0,1:T(8,128)(2,1)S(1)} async-done(((bf16[128,32,128]{2,0,1:T(8,128)(2,1)}), bf16[128,32,128]{2,0,1:T(8,128)(2,1)S(1)}, u32[]{:S(2)}, u32[]{:S(2)}) %all-to-all-start) | async-done | bytes 1048608 | tf_op jit(solution)/shard_map/all_to_all | solution.py:152
  79.9 139.6 %while.59 = (s32[]{:T(128)}, f32[1024,1,128]{2,0,1:T(8,128)S(1)}, f32[1024,1,128]{2,0,1:T(8,128)S(1)}, bf16[4,1024,1,128]{3,1,2,0:T(8,128)(2,1)}, bf16[4,1024,1,...) while((s32[]{:T(128)}, f32[1024,1,128]{2,0,1:T(8,128)S(1)}, ...), condition=%wide.region_6.7_spmd.clone.clone, body=%wide.region_0.6_spmd.clone.clone.sunk | while | flops 1359287296 | bytes 49224388 | solution.py:116
  84.4 28.5 %while.60 = (s32[]{:T(128)}, f32[1024,128]{1,0:T(8,128)S(1)}, f32[1024,128]{1,0:T(8,128)S(1)}, bf16[2,512,1,128]{3,1,0,2:T(8,128)(2,1)}, bf16[2,512,1,128]{3,1,2...) while((s32[]{:T(128)}, f32[1024,128]{1,0:T(8,128)S(1)}, ...), condition=%wide.region_5.5_spmd.clone.clone, body=%wide.region_1.4_spmd.clone.clone.sunk | while | flops 1359025152 | bytes 41875732 | solution.py:104
  109.2 3.1 fusion.81
  119.3 28.5 %while.60 = (s32[]{:T(128)}, f32[1024,128]{1,0:T(8,128)S(1)}, f32[1024,128]{1,0:T(8,128)S(1)}, bf16[2,512,1,128]{3,1,0,2:T(8,128)(2,1)}, bf16[2,512,1,128]{3,1,2...) while((s32[]{:T(128)}, f32[1024,128]{1,0:T(8,128)S(1)}, ...), condition=%wide.region_5.5_spmd.clone.clone, body=%wide.region_1.4_spmd.clone.clone.sunk | while | flops 1359025152 | bytes 41875732 | solution.py:104
  144.1 3.1 fusion.81
  154.2 28.5 %while.60 = (s32[]{:T(128)}, f32[1024,128]{1,0:T(8,128)S(1)}, f32[1024,128]{1,0:T(8,128)S(1)}, bf16[2,512,1,128]{3,1,0,2:T(8,128)(2,1)}, bf16[2,512,1,128]{3,1,2...) while((s32[]{:T(128)}, f32[1024,128]{1,0:T(8,128)S(1)}, ...), condition=%wide.region_5.5_spmd.clone.clone, body=%wide.region_1.4_spmd.clone.clone.sunk | while | flops 1359025152 | bytes 41875732 | solution.py:104
  179.0 3.1 fusion.81
  189.1 28.5 %while.60 = (s32[]{:T(128)}, f32[1024,128]{1,0:T(8,128)S(1)}, f32[1024,128]{1,0:T(8,128)S(1)}, bf16[2,512,1,128]{3,1,0,2:T(8,128)(2,1)}, bf16[2,512,1,128]{3,1,2...) while((s32[]{:T(128)}, f32[1024,128]{1,0:T(8,128)S(1)}, ...), condition=%wide.region_5.5_spmd.clone.clone, body=%wide.region_1.4_spmd.clone.clone.sunk | while | flops 1359025152 | bytes 41875732 | solution.py:104
  213.9 3.1 fusion.81
  221.6 3.4 all-to-all-start.8
  226.6 5.9 %all-to-all-done.8 = bf16[8,2,8192]{2,1,0:T(2,128)(2,1)S(1)} async-done(((bf16[8,2,8192]{2,1,0:T(2,128)(2,1)}), bf16[8,2,8192]{2,1,0:T(2,128)(2,1)S(1)}, u32[]{:S(2)}, u32[]{:S(2)}) %all-to-all-start.8) | async-done | bytes 262176 | tf_op jit(solution)/shard_map/all_to_all | solution.py:172
  232.5 3.6 all-to-all-start.9
  236.1 3.1 copy.153
  239.2 5.6 %all-to-all-done.9 = bf16[8,2,8192]{2,1,0:T(2,128)(2,1)S(1)} async-done(((bf16[8,2,8192]{2,1,0:T(2,128)(2,1)}), bf16[8,2,8192]{2,1,0:T(2,128)(2,1)S(1)}, u32[]{:S(2)}, u32[]{:S(2)}) %all-to-all-start.9) | async-done | bytes 262176 | tf_op jit(solution)/shard_map/all_to_all | solution.py:175
  244.9 3.6 all-to-all-start.6
  250.2 12.6 %all-to-all-done.6 = bf16[1024,4,128]{2,1,0:T(4,128)(2,1)S(1)} async-done(((bf16[1024,4,128]{2,1,0:T(4,128)(2,1)}), bf16[1024,4,128]{2,1,0:T(4,128)(2,1)S(1)}, u32[]{:S(2)}, u32[]{:S(2)}) %all-to-all-start.6) | async-done | bytes 1048608 | tf_op jit(solution)/shard_map/all_to_all | solution.py:168
  262.8 3.9 all-to-all-start.7
  283.2 3.2 copy.163
  296.1 139.9 %all-reduce = (f32[4096]{0:T(1024)S(1)}, f32[512]{0:T(512)S(1)}, f32[512]{0:T(512)S(1)}) all-reduce(f32[4096]{0:T(1024)S(1)} %bitcast.274, f32[512]{0:T(512)S(1)} %bitcast.276, f32[512]{0:T(512)S(1)} %bitcast.277), channel_id=1, replica_groups=mesh['dp'=32,'seq'=8] {'dp'}, use_global_device_ids=true, to_apply=%region_10.11 | all-reduce | flops 5120 | bytes 40960 | tf_op jit(solution)/shard_map/psum | solution.py:184
  436.0 34.5 %all-reduce.1 = (f32[4096]{0:T(1024)}, f32[512]{0:T(512)}, f32[512]{0:T(512)}) all-reduce(f32[4096]{0:T(1024)S(1)} %get-tuple-element.709, f32[512]{0:T(512)S(1)} %get-tuple-element.710, f32[512]{0:T(512)S(1)} %get-tuple-element.711), channel_id=1, replica_groups=mesh['dp'=32,'seq'=8] {'seq'}, use_global_device_ids=true, to_apply=%region_11.12 | all-reduce | flops 5120 | bytes 40960 | tf_op jit(solution)/shard_map/psum | solution.py:183
  (323 shorter events, 160.8 us)
Async XLA Ops:
  0.6 8.4 %copy-start.22 = (bf16[1,128,512]{2,1,0:T(8,128)(2,1)S(1)}, bf16[1,128,512]{2,1,0:T(8,128)(2,1)}, u32[]{:S(2)}) copy-start(bf16[1,128,512]{2,1,0:T(8,128)(2,1)} %param.15) | copy-start | bytes 393220
  0.6 8.6 %copy-start.23 = (bf16[1,128,512]{2,1,0:T(8,128)(2,1)S(1)}, bf16[1,128,512]{2,1,0:T(8,128)(2,1)}, u32[]{:S(2)}) copy-start(bf16[1,128,512]{2,1,0:T(8,128)(2,1)} %param.18) | copy-start | bytes 393220
  2.4 15.7 %copy-start.25 = (bf16[512]{0:T(512)(128)(2,1)S(1)}, bf16[512]{0:T(512)(128)(2,1)}, u32[]{:S(2)}) copy-start(bf16[512]{0:T(512)(128)(2,1)} %param.20) | copy-start | bytes 3076
  2.4 11.5 %all-to-all-start.2 = ((bf16[128,8,128]{2,0,1:T(8,128)(2,1)}), bf16[128,8,128]{2,0,1:T(8,128)(2,1)S(1)}, u32[]{:S(2)}, u32[]{:S(2)}) async-start(bf16[128,8,128]{2,0,1:T(8,128)(2,1)} %bitcast.11), calls=%async_computation.2 | async-start | bytes 524288 | tf_op jit(solution)/shard_map/all_to_all | solution.py:158
  9.8 42.0 %copy-start.8 = (f32[128,128]{1,0:T(8,128)}, f32[128,128]{1,0:T(8,128)S(1)}, u32[]{:S(2)}) copy-start(f32[128,128]{1,0:T(8,128)S(1)} %get-tuple-element.738) | copy-start | bytes 196612
  9.8 42.1 %copy-start.6 = (f32[128,128]{1,0:T(8,128)}, f32[128,128]{1,0:T(8,128)S(1)}, u32[]{:S(2)}) copy-start(f32[128,128]{1,0:T(8,128)S(1)} %get-tuple-element.737) | copy-start | bytes 196612
  14.6 10.6 %all-to-all-start.4 = ((bf16[128,8,128]{2,0,1:T(8,128)(2,1)}), bf16[128,8,128]{2,0,1:T(8,128)(2,1)S(1)}, u32[]{:S(2)}, u32[]{:S(2)}) async-start(bf16[128,8,128]{2,0,1:T(8,128)(2,1)} %bitcast.21), calls=%async_computation.4 | async-start | bytes 524288 | tf_op jit(solution)/shard_map/all_to_all | solution.py:159
  18.1 22.8 %copy-start.10 = (bf16[1,128,4096]{2,1,0:T(8,128)(2,1)S(1)}, bf16[1,128,4096]{2,1,0:T(8,128)(2,1)}, u32[]{:S(2)}) copy-start(bf16[1,128,4096]{2,1,0:T(8,128)(2,1)} %param.23) | copy-start | bytes 3145732
  25.3 17.0 %copy-start.13 = (bf16[128,8,128]{2,0,1:T(8,128)(2,1)}, bf16[128,8,128]{2,0,1:T(8,128)(2,1)S(1)}, u32[]{:S(2)}) copy-start(bf16[128,8,128]{2,0,1:T(8,128)(2,1)S(1)} %all-to-all-done.4) | copy-start | bytes 786436
  26.1 10.6 %all-to-all-start.5 = ((bf16[128,8,128]{2,0,1:T(8,128)(2,1)}), bf16[128,8,128]{2,0,1:T(8,128)(2,1)S(1)}, u32[]{:S(2)}, u32[]{:S(2)}) async-start(bf16[128,8,128]{2,0,1:T(8,128)(2,1)} %bitcast.26), calls=%async_computation.5 | async-start | bytes 524288 | tf_op jit(solution)/shard_map/all_to_all | solution.py:154
  37.5 10.6 %all-to-all-start.3 = ((bf16[128,8,128]{2,0,1:T(8,128)(2,1)}), bf16[128,8,128]{2,0,1:T(8,128)(2,1)S(1)}, u32[]{:S(2)}, u32[]{:S(2)}) async-start(bf16[128,8,128]{2,0,1:T(8,128)(2,1)} %bitcast.17), calls=%async_computation.3 | async-start | bytes 524288 | tf_op jit(solution)/shard_map/all_to_all | solution.py:153
  40.9 11.1 %copy-start.11 = (bf16[1,128,4096]{2,1,0:T(8,128)(2,1)S(1)}, bf16[1,128,4096]{2,1,0:T(8,128)(2,1)}, u32[]{:S(2)}) copy-start(bf16[1,128,4096]{2,1,0:T(8,128)(2,1)} %param.14) | copy-start | bytes 3145732
  48.1 3.8 copy-start.17
  48.1 4.6 copy-start.24
  48.2 15.5 %all-to-all-start.1 = ((bf16[128,32,128]{0,2,1:T(8,128)(2,1)}), bf16[128,32,128]{0,2,1:T(8,128)(2,1)S(1)}, u32[]{:S(2)}, u32[]{:S(2)}) async-start(bf16[128,32,128]{0,2,1:T(8,128)(2,1)} %bitcast.6), calls=%async_computation.1 | async-start | bytes 2097152 | tf_op jit(solution)/shard_map/all_to_all | solution.py:155
  54.5 12.8 %copy-start.14 = (bf16[128,8,128]{2,0,1:T(8,128)(2,1)S(1)}, bf16[128,8,128]{2,0,1:T(8,128)(2,1)}, u32[]{:S(2)}) copy-start(bf16[128,8,128]{2,0,1:T(8,128)(2,1)} %copy-done.13) | copy-start | bytes 786436
  54.5 12.8 %copy-start.16 = (bf16[128,8,128]{2,0,1:T(8,128)(2,1)S(1)}, bf16[128,8,128]{2,0,1:T(8,128)(2,1)}, u32[]{:S(2)}) copy-start(bf16[128,8,128]{2,0,1:T(8,128)(2,1)} %copy-done.15) | copy-start | bytes 786436
  63.7 15.0 %all-to-all-start = ((bf16[128,32,128]{2,0,1:T(8,128)(2,1)}), bf16[128,32,128]{2,0,1:T(8,128)(2,1)S(1)}, u32[]{:S(2)}, u32[]{:S(2)}) async-start(bf16[128,32,128]{2,0,1:T(8,128)(2,1)} %copy.142), calls=%async_computation | async-start | bytes 2097152 | tf_op jit(solution)/shard_map/all_to_all | solution.py:152
  94.3 3.7 copy-start
  108.5 3.7 copy-start
  129.2 3.7 copy-start
  143.4 3.7 copy-start
  164.1 3.7 copy-start
  178.3 3.7 copy-start
  199.0 3.7 copy-start
  213.2 3.7 copy-start
  221.6 10.9 %all-to-all-start.8 = ((bf16[8,2,8192]{2,1,0:T(2,128)(2,1)}), bf16[8,2,8192]{2,1,0:T(2,128)(2,1)S(1)}, u32[]{:S(2)}, u32[]{:S(2)}) async-start(bf16[8,2,8192]{2,1,0:T(2,128)(2,1)} %reshape.436), calls=%async_computation.8 | async-start | bytes 524288 | tf_op jit(solution)/shard_map/all_to_all | solution.py:172
  232.5 12.4 %all-to-all-start.9 = ((bf16[8,2,8192]{2,1,0:T(2,128)(2,1)}), bf16[8,2,8192]{2,1,0:T(2,128)(2,1)S(1)}, u32[]{:S(2)}, u32[]{:S(2)}) async-start(bf16[8,2,8192]{2,1,0:T(2,128)(2,1)} %reshape.438), calls=%async_computation.9 | async-start | bytes 524288 | tf_op jit(solution)/shard_map/all_to_all | solution.py:175
  236.1 12.3 %copy-start.12 = (bf16[4,1024,1,128]{3,1,2,0:T(8,128)(2,1)S(1)}, bf16[4,1024,1,128]{3,1,2,0:T(8,128)(2,1)}, u32[]{:S(2)}) copy-start(bf16[4,1024,1,128]{3,1,2,0:T(8,128)(2,1)} %get-tuple-element.348) | copy-start | bytes 3145732
  244.9 17.9 %all-to-all-start.6 = ((bf16[1024,4,128]{2,1,0:T(4,128)(2,1)}), bf16[1024,4,128]{2,1,0:T(4,128)(2,1)S(1)}, u32[]{:S(2)}, u32[]{:S(2)}) async-start(bf16[1024,4,128]{2,1,0:T(4,128)(2,1)} %copy.153), calls=%async_computation.6 | async-start | bytes 2097152 | tf_op jit(solution)/shard_map/all_to_all | solution.py:168
  262.8 15.5 %all-to-all-start.7 = ((bf16[1024,4,128]{2,1,0:T(4,128)(2,1)}), bf16[1024,4,128]{2,1,0:T(4,128)(2,1)S(1)}, u32[]{:S(2)}, u32[]{:S(2)}) async-start(bf16[1024,4,128]{2,1,0:T(4,128)(2,1)} %bitcast.260), calls=%async_computation.7 | async-start | bytes 2097152 | tf_op jit(solution)/shard_map/all_to_all | solution.py:169
  267.1 5.0 %copy-start.9 = (f32[128,128]{1,0:T(8,128)S(1)}, f32[128,128]{1,0:T(8,128)}, u32[]{:S(2)}) copy-start(f32[128,128]{1,0:T(8,128)} %copy-done.8) | copy-start | bytes 196612
  (17 other events, 30.5 us)
